TPU v7x, 512 devices: a whole 4x8x8 slice. The times are simulated.
512 devices in a mesh: bulk: 128 (over y, z, core), rep: 4 (over x).
Axes of the slice: x: 4, y: 8, z: 8, core: 2. Of those that a mesh axis runs over, the one named last changes fastest.
Arguments:
- orbitals: float32 [16384, 2048], P('rep', 'bulk'), may hold values from -6 to 6
- triangles: float32 [1024, 1024], P('rep', 'bulk'), may hold values from -0.09375 to 0.09375
- coupling: float32 [1024, 1024], P('rep', 'bulk'), may hold values from -0.09375 to 0.09375
- diagonals: float32 [2, 1024], P(None, 'bulk'), may hold values from 1 to 2
Outputs:
- solved: float32 [16384, 2048], P(('rep', 'bulk'))
All inputs are finite; a program needn't handle non-finite values.
Results may differ from a plain program's by a relative error of at most 0.000084.
Values sent between devices are 32-bit elements; how exact they have to be, the bound alone decides.
A program may use at most 64 MiB of HBM per device.

v0:
```python
import jax
import jax.numpy as jnp
from jax import lax
from jax.sharding import PartitionSpec as P


def unpack(triangles, diagonals):
    first_block = jnp.tril(triangles, -1) + jnp.diag(diagonals[0])
    second_block = jnp.tril(triangles.T, -1) + jnp.diag(diagonals[1])
    return (first_block, second_block)


def per_device(orbitals, triangles, coupling, diagonals):
    tri_rows, couple_rows = (
        lax.all_gather(triangles, "rep", axis=0, tiled=True),
        lax.all_gather(coupling, "rep", axis=0, tiled=True),
    )
    tri_whole, couple_whole, diag_whole = (
        lax.all_gather(tri_rows, "bulk", axis=1, tiled=True),
        lax.all_gather(couple_rows, "bulk", axis=1, tiled=True),
        lax.all_gather(diagonals, "bulk", axis=1, tiled=True),
    )
    first_block, second_block = unpack(tri_whole, diag_whole)
    panel = first_block.shape[0]
    groups = lax.axis_size("bulk")
    local_rows = orbitals.shape[0] // groups
    blocks = orbitals.reshape(groups, local_rows, orbitals.shape[1])
    received = lax.all_to_all(blocks, "bulk", split_axis=0, concat_axis=2, tiled=True)
    count = received.shape[1]
    full_width = received.shape[2]
    rows_now = received.reshape(count, full_width)
    left_part = rows_now[:, :panel]
    right_part = rows_now[:, panel:]
    solved_one = jax.scipy.linalg.solve_triangular(first_block, left_part.T, lower=True).T
    update = jnp.dot(
        solved_one,
        couple_whole.T,
        precision=lax.Precision.HIGHEST,
        preferred_element_type=jnp.float32,
    )
    solved_two = jax.scipy.linalg.solve_triangular(
        second_block, (right_part - update).T, lower=True
    ).T
    joined = jnp.concatenate([solved_one, solved_two], axis=1)
    result = joined.reshape(1, count, full_width)
    return result.reshape(local_rows, result.shape[2])


def solution(mesh):
    return jax.shard_map(
        per_device,
        mesh=mesh,
        in_specs=(P("rep", "bulk"), P("rep", "bulk"), P("rep", "bulk"), P(None, "bulk")),
        out_specs=P(("rep", "bulk"), None),
        check_vma=False,
    )
```

profile of v0, /device:TPU:1, one launch (start us, length us, event | category | flops | bytes accessed | tf_op | source)
XLA Modules:
  0.0 365.9 jit_solution(3939326885254710032)
XLA Ops:
  6.5 11.9 %all_gather.15 = f32[1024,8]{0,1:T(8,128)} all-gather(f32[256,8]{0,1:T(8,128)} %param.7), channel_id=1, replica_groups=mesh['bulk'=128,'rep'=4] {'rep'}, dimensions={0}, use_global_device_ids=true | all-gather | bytes 40960 | tf_op jit(solution)/shard_map/all_gather | solution.py:15
  18.5 1.3 reshape.27
  20.4 1.2 reshape.53
  21.6 20.3 %all-to-all-start = ((f32[128,1,512]{2,1,0:T(1,128)}), f32[128,1,512]{2,1,0:T(1,128)S(1)}, u32[]{:S(2)}, u32[]{:S(2)}) async-start(f32[128,1,512]{2,1,0:T(1,128)} %reshape.53), calls=%async_computation | async-start | bytes 524288 | tf_op jit(solution)/shard_map/all_to_all | solution.py:28
  41.9 10.3 %all_gather.18 = f32[1024,8]{0,1:T(8,128)} all-gather(f32[256,8]{0,1:T(8,128)S(1)} %copy-done.1), channel_id=1, replica_groups=mesh['bulk'=128,'rep'=4] {'rep'}, dimensions={0}, use_global_device_ids=true | all-gather | bytes 40960 | tf_op jit(solution)/shard_map/all_gather | solution.py:16
  53.1 53.9 %all-gather = f32[128,8,2]{1,2,0:T(2,128)S(1)} all-gather(f32[1,8,2]{1,2,0:T(2,128)S(1)} %bitcast.165), channel_id=1, replica_groups=mesh['bulk'=128,'rep'=4] {'bulk'}, dimensions={0}, use_global_device_ids=true | all-gather | bytes 8256 | tf_op jit(solution)/shard_map/all_gather | solution.py:21
  107.1 2.0 copy.25
  109.3 2.0 copy.26
  112.6 2.2 reduce
  115.1 1.1 fusion.71
  116.2 1.2 copy.30
  117.4 1.2 copy.29
  118.7 5.0 %add_select_fusion = f32[1024,1024]{0,1:T(8,128)} fusion(f32[1024,1024]{0,1:T(8,128)} %all-gather.4.cloned.1.call-done, f32[1024]{0:T(1024)S(1)} %bitcast.163, s32[1024]{0:T(1024)S(1)} %iota_add_fusion), kind=kLoop, calls=%fused_computation.9 | loop fusion | flops 7340032 | bytes 8396800 | tf_op jit(solution)/shard_map/jit(_solve_triangular)/triangular_solve | solution.py:34
  123.7 23.5 %while.4 = (s32[]{:T(128)}, f32[1024,1024]{0,1:T(8,128)}, s32[8,2]{0,1:T(2,128)S(1)}, f32[8,128,128]{2,1,0:T(8,128)S(1)}, s32[]{:T(128)}) while((s32[]{:T(128)}, f32[1024,1024]{0,1:T(8,128)}, s32[8,2]{0,1:T(2,128)S(1)}, f32[8,128,128]{2,1,0:T(8,128)S(1)}, s32[]{:T(128)}) %tuple.84), condition=%wide.while_cond, body=%wide.while_body.sunk | while | flops 2 | bytes 393329 | solution.py:34
  124.3 2.2 dynamic-slice.13
  127.2 2.2 dynamic-slice.13
  130.2 2.2 dynamic-slice.13
  133.1 2.2 dynamic-slice.13
  136.0 2.2 dynamic-slice.13
  139.0 2.2 dynamic-slice.13
  141.9 2.2 dynamic-slice.13
  144.9 2.1 dynamic-slice.13
  147.1 78.6 %custom-call.4 = f32[8,128,128]{1,2,0:T(8,128)S(1)} custom-call(f32[8,128,128]{2,1,0:T(8,128)S(1)} %get-tuple-element.20), custom_call_target="InvertDiagBlocksLowerTriangular" | custom-call | tf_op jit(solution)/shard_map/jit(_solve_triangular)/triangular_solve | solution.py:34
  225.7 5.1 %fusion.1 = f32[1024,1024]{1,0:T(8,128)} fusion(pred[1024,1024]{1,0:T(8,128)(4,1)S(1)} %copy.25, f32[1024,1024]{0,1:T(8,128)} %all-gather.4.cloned.1.call-done, pred[1024,1024]{1,0:T(8,128)(4,1)S(1)} %copy.26, f32[1024]{0:T(1024)S(1)} %bitcast.164), kind=kLoop, calls=%fused_computation.6 | loop fusion | flops 5242880 | bytes 10489856 | tf_op jit(solution)/shard_map/jit(_solve_triangular)/triangular_solve | solution.py:41
  230.8 23.2 %while.5 = (s32[]{:T(128)}, f32[1024,1024]{1,0:T(8,128)}, s32[8,2]{0,1:T(2,128)S(1)}, f32[8,128,128]{2,1,0:T(8,128)S(1)}, s32[]{:T(128)}) while((s32[]{:T(128)}, f32[1024,1024]{1,0:T(8,128)}, s32[8,2]{0,1:T(2,128)S(1)}, f32[8,128,128]{2,1,0:T(8,128)S(1)}, s32[]{:T(128)}) %tuple.94), condition=%wide.while_cond.clone, body=%wide.while_body.clone.sunk | while | flops 2 | bytes 131189 | solution.py:41
  231.5 2.3 bitcast_dynamic-update-slice_fusion.5
  234.4 2.3 bitcast_dynamic-update-slice_fusion.5
  237.3 2.3 bitcast_dynamic-update-slice_fusion.5
  240.2 2.3 bitcast_dynamic-update-slice_fusion.5
  243.1 2.3 bitcast_dynamic-update-slice_fusion.5
  246.0 2.3 bitcast_dynamic-update-slice_fusion.5
  248.9 2.3 bitcast_dynamic-update-slice_fusion.5
  251.8 2.2 bitcast_dynamic-update-slice_fusion.5
  254.1 78.8 %custom-call.5 = f32[8,128,128]{1,2,0:T(8,128)S(1)} custom-call(f32[8,128,128]{2,1,0:T(8,128)S(1)} %get-tuple-element.21), custom_call_target="InvertDiagBlocksLowerTriangular" | custom-call | tf_op jit(solution)/shard_map/jit(_solve_triangular)/triangular_solve | solution.py:41
  334.3 1.1 convolution_subtract_fusion.7
  335.5 1.2 convolution_subtract_fusion.6
  336.9 1.2 convolution_subtract_fusion.5
  338.3 1.3 convolution_subtract_fusion.14
  339.8 1.3 convolution_subtract_fusion.13
  341.3 1.4 convolution_subtract_fusion.12
  342.9 4.7 %fusion.2 = f32[1024,32]{0,1:T(8,128)S(1)} fusion(f32[32,1024]{1,0:T(8,128)S(1)} %copy.30, f32[1024,32]{0,1:T(8,128)S(1)} %convolution_dynamic-update-slice_fusion.1, f32[1024,1024]{0,1:T(8,128)} %all-gather.6.cloned.1.call-done), kind=kOutput, calls=%fused_computation.13 | convolution fusion | flops 402685952 | bytes 4587520 | tf_op jit(solution)/shard_map/dot_general | solution.py:35
  347.8 1.0 convolution_subtract_fusion.4
  349.0 1.1 convolution_subtract_fusion.3
  350.3 1.3 convolution_subtract_fusion.2
  351.8 1.3 convolution_subtract_fusion.1
  353.3 1.4 convolution_subtract_fusion.11
  354.9 1.5 convolution_subtract_fusion.10
  356.5 1.6 convolution_subtract_fusion.9
  (92 shorter events, 18.5 us)
Async XLA Ops:
  6.5 35.3 %copy-start.1 = (f32[256,8]{0,1:T(8,128)S(1)}, f32[256,8]{0,1:T(8,128)}, u32[]{:S(2)}) copy-start(f32[256,8]{0,1:T(8,128)} %param.8) | copy-start | bytes 24580
  6.5 46.5 %copy-start.2 = (f32[2,8]{1,0:T(2,128)S(1)}, f32[2,8]{1,0:T(2,128)}, u32[]{:S(2)}) copy-start(f32[2,8]{1,0:T(2,128)} %param.9) | copy-start | bytes 196
  6.5 112.1 %all-gather.4.cloned.1.call-start = ((), (), s32[]{:S(2)}) async-start(), calls=%async_computation.1 | async-start | bytes 4227072 | tf_op jit(solution)/shard_map/all_gather | solution.py:19
  21.6 89.8 %all-to-all-start = ((f32[128,1,512]{2,1,0:T(1,128)}), f32[128,1,512]{2,1,0:T(1,128)S(1)}, u32[]{:S(2)}, u32[]{:S(2)}) async-start(f32[128,1,512]{2,1,0:T(1,128)} %reshape.53), calls=%async_computation | async-start | bytes 524288 | tf_op jit(solution)/shard_map/all_to_all | solution.py:28
  41.8 301.1 %all-gather.6.cloned.1.call-start = ((), (), s32[]{:S(2)}) async-start(), calls=%async_computation.2 | async-start | bytes 4227072 | tf_op jit(solution)/shard_map/all_gather | solution.py:20
  111.4 0.7 copy-start
Sparse Core Ops, SparseCore 0:
  18.6 93.3 all-gather.3
  115.1 82.0 all-gather.5
where the time goes:
time: 368 us; the launch traced here: 366 us
  other arithmetic  171 us (46%)
  blocking collectives  76.1 us (21%)
  local copies, waits for them, and re-layouts  58.5 us (16%)
  matrix products  25.1 us (7%)
  starting transfers between devices  20.3 us (6%)
  between operations  13.8 us (4%)
    another operation x2, other arithmetic, per_device(): jax.scipy.linalg.solve_triangular(second_block, (right_part - update).T,...  83.9 us
    another operation x3, other arithmetic, per_device(): jax.scipy.linalg.solve_triangular(first_block, left_part.T, lower=True)  83.5 us
    all_gather x1, blocking collectives, per_device(): lax.all_gather(diagonals, 'bulk', axis=1, tiled=True)  53.9 us
    another operation x43, local copies, waits for them, and re-layouts, per_device(): jax.scipy.linalg.solve_triangular(first_block, left_part.T, lower=True)  23.3 us
    another operation x24, local copies, waits for them, and re-layouts, per_device(): jax.scipy.linalg.solve_triangular(second_block, (right_part - update).T,...  23.1 us
    all_to_all x1, starting transfers between devices, per_device(): lax.all_to_all(blocks, 'bulk', split_axis=0, concat_axis=2, tiled=True)  20.3 us
    all_gather x1, blocking collectives, per_device(): lax.all_gather(triangles, 'rep', axis=0, tiled=True)  11.9 us
    another operation x15, matrix products, per_device(): jax.scipy.linalg.solve_triangular(second_block, (right_part - update).T,...  10.6 us
  transfers between devices with their start and end apart: 3, of which 0 were waited for; matrix products, arithmetic and copies ran while one was open for 65% of the time, Pallas kernels for 0%

commit v1 on v0

--- a/solution.py
+++ b/solution.py
@@ -25,7 +25,9 @@
     groups = lax.axis_size("bulk")
     local_rows = orbitals.shape[0] // groups
     blocks = orbitals.reshape(groups, local_rows, orbitals.shape[1])
-    received = lax.all_to_all(blocks, "bulk", split_axis=0, concat_axis=2, tiled=True)
+    pieces = jnp.split(blocks, lax.axis_size("bulk"), axis=0)
+    got = lax.all_to_all(jnp.stack(pieces), "bulk", 0, 0)
+    received = jnp.concatenate(got, axis=2)
     count = received.shape[1]
     full_width = received.shape[2]
     rows_now = received.reshape(count, full_width)

time: 368 us -> 469 us (1.27)
  local copies, waits for them, and re-layouts: 58.5 us -> 155 us
    unnamed x11 -> x136, local copies, waits for them, and re-layouts: 4.67 us -> 100 us
  transfers between devices with their start and end apart: 3 -> 3, of which waited for: 0 -> 0; matrix products, arithmetic and copies ran while one was open for 65% -> 72% of each run, Pallas kernels for 0% -> 0%
where the time goes in v1:
time: 469 us; the launch traced here: 462 us
  other arithmetic  172 us (37%)
  local copies, waits for them, and re-layouts  155 us (33%)
  blocking collectives  76.4 us (16%)
  matrix products  25.1 us (5%)
  starting transfers between devices  20.1 us (4%)
  between operations  13.9 us (3%)
    unnamed x136, local copies, waits for them, and re-layouts  100 us
    another operation x2, other arithmetic, per_device(): jax.scipy.linalg.solve_triangular(second_block, (right_part - update).T,...  83.9 us
    another operation x3, other arithmetic, per_device(): jax.scipy.linalg.solve_triangular(first_block, left_part.T, lower=True)  83.6 us
    all_gather x1, blocking collectives, per_device(): lax.all_gather(diagonals, 'bulk', axis=1, tiled=True)  53.6 us
    another operation x43, local copies, waits for them, and re-layouts, per_device(): jax.scipy.linalg.solve_triangular(first_block, left_part.T, lower=True)  24.7 us
    another operation x24, local copies, waits for them, and re-layouts, per_device(): jax.scipy.linalg.solve_triangular(second_block, (right_part - update).T,...  23.4 us
    all_to_all x1, starting transfers between devices, per_device(): got = lax.all_to_all(jnp.stack(pieces), 'bulk', 0, 0)  20 us
    all_gather x1, blocking collectives, per_device(): lax.all_gather(triangles, 'rep', axis=0, tiled=True)  12.1 us
  transfers between devices with their start and end apart: 3, of which 0 were waited for; matrix products, arithmetic and copies ran while one was open for 72% of the time, Pallas kernels for 0%

profile of v1, /device:TPU:1, one launch (start us, length us, event | category | flops | bytes accessed | tf_op | source)
XLA Modules:
  0.0 462.3 jit_solution(5996929328359170207)
XLA Ops:
  6.5 12.1 %all_gather.15 = f32[1024,8]{0,1:T(8,128)} all-gather(f32[256,8]{0,1:T(8,128)} %param.7), channel_id=1, replica_groups=mesh['bulk'=128,'rep'=4] {'rep'}, dimensions={0}, use_global_device_ids=true | all-gather | bytes 40960 | tf_op jit(solution)/shard_map/all_gather | solution.py:15
  115.0 1.2 reshape.305
  116.1 20.0 %all-to-all-start = ((f32[128,1,512]{2,1,0:T(1,128)}), f32[128,1,512]{2,1,0:T(1,128)S(1)}, u32[]{:S(2)}, u32[]{:S(2)}) async-start(f32[128,1,512]{2,1,0:T(1,128)} %reshape.305), calls=%async_computation | async-start | bytes 524288 | tf_op jit(solution)/shard_map/all_to_all | solution.py:29
  136.2 10.7 %all_gather.18 = f32[1024,8]{0,1:T(8,128)} all-gather(f32[256,8]{0,1:T(8,128)} %param.8), channel_id=1, replica_groups=mesh['bulk'=128,'rep'=4] {'rep'}, dimensions={0}, use_global_device_ids=true | all-gather | bytes 40960 | tf_op jit(solution)/shard_map/all_gather | solution.py:16
  147.8 53.6 %all-gather = f32[128,8,2]{1,2,0:T(2,128)S(1)} all-gather(f32[1,8,2]{1,2,0:T(2,128)S(1)} %bitcast.415), channel_id=1, replica_groups=mesh['bulk'=128,'rep'=4] {'bulk'}, dimensions={0}, use_global_device_ids=true | all-gather | bytes 8256 | tf_op jit(solution)/shard_map/all_gather | solution.py:21
  201.6 2.0 copy.572
  203.9 2.0 copy.573
  207.1 2.2 reduce
  209.6 1.1 fusion.71
  210.8 1.2 copy.577
  212.0 1.3 copy.576
  213.3 5.0 %add_select_fusion = f32[1024,1024]{0,1:T(8,128)} fusion(f32[1024,1024]{0,1:T(8,128)} %all-gather.4.cloned.1.call-done, f32[1024]{0:T(1024)S(1)} %bitcast.413, s32[1024]{0:T(1024)S(1)} %iota_add_fusion), kind=kLoop, calls=%fused_computation.9 | loop fusion | flops 7340032 | bytes 8396800 | tf_op jit(solution)/shard_map/jit(_solve_triangular)/triangular_solve | solution.py:36
  218.3 24.9 %while.4 = (s32[]{:T(128)}, f32[1024,1024]{0,1:T(8,128)}, s32[8,2]{0,1:T(2,128)S(1)}, f32[8,128,128]{2,1,0:T(8,128)S(1)}, s32[]{:T(128)}) while((s32[]{:T(128)}, f32[1024,1024]{0,1:T(8,128)}, s32[8,2]{0,1:T(2,128)S(1)}, f32[8,128,128]{2,1,0:T(8,128)S(1)}, s32[]{:T(128)}) %tuple.88), condition=%wide.while_cond, body=%wide.while_body.sunk | while | flops 2 | bytes 393329 | solution.py:36
  219.0 2.3 dynamic-slice.13
  222.1 2.3 dynamic-slice.13
  225.2 2.3 dynamic-slice.13
  228.3 2.3 dynamic-slice.13
  231.4 2.3 dynamic-slice.13
  234.6 2.3 dynamic-slice.13
  237.7 2.3 dynamic-slice.13
  240.8 2.3 dynamic-slice.13
  243.2 78.6 %custom-call.4 = f32[8,128,128]{1,2,0:T(8,128)S(1)} custom-call(f32[8,128,128]{2,1,0:T(8,128)S(1)} %get-tuple-element.20), custom_call_target="InvertDiagBlocksLowerTriangular" | custom-call | tf_op jit(solution)/shard_map/jit(_solve_triangular)/triangular_solve | solution.py:36
  321.8 5.1 %fusion.1 = f32[1024,1024]{1,0:T(8,128)} fusion(pred[1024,1024]{1,0:T(8,128)(4,1)S(1)} %copy.572, f32[1024,1024]{0,1:T(8,128)} %all-gather.4.cloned.1.call-done, pred[1024,1024]{1,0:T(8,128)(4,1)S(1)} %copy.573, f32[1024]{0:T(1024)S(1)} %bitcast.414), kind=kLoop, calls=%fused_computation.6 | loop fusion | flops 5242880 | bytes 10489856 | tf_op jit(solution)/shard_map/jit(_solve_triangular)/triangular_solve | solution.py:43
  326.9 23.6 %while.5 = (s32[]{:T(128)}, f32[1024,1024]{1,0:T(8,128)}, s32[8,2]{0,1:T(2,128)S(1)}, f32[8,128,128]{2,1,0:T(8,128)S(1)}, s32[]{:T(128)}) while((s32[]{:T(128)}, f32[1024,1024]{1,0:T(8,128)}, s32[8,2]{0,1:T(2,128)S(1)}, f32[8,128,128]{2,1,0:T(8,128)S(1)}, s32[]{:T(128)}) %tuple.98), condition=%wide.while_cond.clone, body=%wide.while_body.clone.sunk | while | flops 2 | bytes 131189 | solution.py:43
  327.5 2.3 bitcast_dynamic-update-slice_fusion.5
  330.5 2.3 bitcast_dynamic-update-slice_fusion.5
  333.5 2.3 bitcast_dynamic-update-slice_fusion.5
  336.4 2.3 bitcast_dynamic-update-slice_fusion.5
  339.4 2.3 bitcast_dynamic-update-slice_fusion.5
  342.3 2.3 bitcast_dynamic-update-slice_fusion.5
  345.3 2.3 bitcast_dynamic-update-slice_fusion.5
  348.2 2.2 bitcast_dynamic-update-slice_fusion.5
  350.5 78.8 %custom-call.5 = f32[8,128,128]{1,2,0:T(8,128)S(1)} custom-call(f32[8,128,128]{2,1,0:T(8,128)S(1)} %get-tuple-element.21), custom_call_target="InvertDiagBlocksLowerTriangular" | custom-call | tf_op jit(solution)/shard_map/jit(_solve_triangular)/triangular_solve | solution.py:43
  429.5 1.0 convolution_subtract_fusion.8
  430.7 1.1 convolution_subtract_fusion.7
  432.0 1.2 convolution_subtract_fusion.6
  433.3 1.2 convolution_subtract_fusion.5
  434.7 1.3 convolution_subtract_fusion.14
  436.2 1.3 convolution_subtract_fusion.13
  437.7 1.4 convolution_subtract_fusion.12
  439.3 4.7 %fusion.2 = f32[1024,32]{0,1:T(8,128)S(1)} fusion(f32[32,1024]{1,0:T(8,128)S(1)} %copy.577, f32[1024,32]{0,1:T(8,128)S(1)} %convolution_dynamic-update-slice_fusion.1, f32[1024,1024]{0,1:T(8,128)} %all-gather.6.cloned.1.call-done), kind=kOutput, calls=%fused_computation.13 | convolution fusion | flops 402685952 | bytes 4587520 | tf_op jit(solution)/shard_map/dot_general | solution.py:37
  444.2 1.0 convolution_subtract_fusion.4
  445.4 1.1 convolution_subtract_fusion.3
  446.8 1.3 convolution_subtract_fusion.2
  448.2 1.3 convolution_subtract_fusion.1
  449.7 1.4 convolution_subtract_fusion.11
  451.3 1.5 convolution_subtract_fusion.10
  452.9 1.6 convolution_subtract_fusion.9
  (216 shorter events, 114.0 us)
Async XLA Ops:
  6.5 141.2 %copy-start.1 = (f32[2,8]{1,0:T(2,128)S(1)}, f32[2,8]{1,0:T(2,128)}, u32[]{:S(2)}) copy-start(f32[2,8]{1,0:T(2,128)} %param.9) | copy-start | bytes 196
  6.5 206.7 %all-gather.4.cloned.1.call-start = ((), (), s32[]{:S(2)}) async-start(), calls=%async_computation.1 | async-start | bytes 4227072 | tf_op jit(solution)/shard_map/all_gather | solution.py:19
  116.1 89.7 %all-to-all-start = ((f32[128,1,512]{2,1,0:T(1,128)}), f32[128,1,512]{2,1,0:T(1,128)S(1)}, u32[]{:S(2)}, u32[]{:S(2)}) async-start(f32[128,1,512]{2,1,0:T(1,128)} %reshape.305), calls=%async_computation | async-start | bytes 524288 | tf_op jit(solution)/shard_map/all_to_all | solution.py:29
  136.2 303.1 %all-gather.6.cloned.1.call-start = ((), (), s32[]{:S(2)}) async-start(), calls=%async_computation.2 | async-start | bytes 4227072 | tf_op jit(solution)/shard_map/all_gather | solution.py:20
  205.9 0.7 copy-start
Sparse Core Ops, SparseCore 0:
  18.8 91.2 all-gather.3
  147.1 86.9 all-gather.5
